TPU v7x, 32 devices: a whole 2x2x4 slice. The times are simulated.
32 devices in a mesh: expert: 8 (over z, y), ctx: 4 (over x, core).
Axes of the slice: x: 2, y: 2, z: 4, core: 2. Of those that a mesh axis runs over, the one named last changes fastest.
Arguments:
- resid: bfloat16 [4096, 2048], P(('expert', 'ctx')), may hold values from -30 to 30
- queries: bfloat16 [4096, 2048], P(('expert', 'ctx')), may hold values from -8 to 8
- keys: bfloat16 [4096, 2048], P(('expert', 'ctx')), may hold values from -8 to 8
- values: bfloat16 [4096, 2048], P(('expert', 'ctx')), may hold values from -6 to 6
- mod_scale: float32 [8, 2048], P('expert'), may hold values from -0.5 to 0.5
- mod_shift: float32 [8, 2048], P('expert'), may hold values from -3 to 3
- mod_gate: float32 [8, 2048], P('expert'), may hold values from 0.5 to 1.5
- router: bfloat16 [2048, 8], replicated, may hold values from -0.125 to 0.125
- w_in: bfloat16 [8, 2048, 1024], P('expert', None, 'ctx'), may hold values from -0.125 to 0.125
- w_out: bfloat16 [8, 1024, 2048], P('expert', 'ctx'), may hold values from -0.1875 to 0.1875
- expert_ids: int32 [4096, 2], P(('expert', 'ctx')), may hold values from 0 to 7, all different within a row; in each aligned block of 128 rows (0 to 127, 128 to 255, ...) at most 40 rows name the same one
- grad_out: bfloat16 [4096, 2048], P(('expert', 'ctx')), may hold values from -1.5 to 1.5
Outputs:
- mixed_out: bfloat16 [4096, 2048], P(('expert', 'ctx'))
- resid_grad: bfloat16 [4096, 2048], P(('expert', 'ctx'))
- grad_queries: bfloat16 [4096, 2048], P(('expert', 'ctx'))
- grad_keys: bfloat16 [4096, 2048], P(('expert', 'ctx'))
- grad_values: bfloat16 [4096, 2048], P(('expert', 'ctx'))
- grad_w_in: bfloat16 [8, 2048, 1024], P('expert', None, 'ctx')
- grad_w_out: bfloat16 [8, 1024, 2048], P('expert', 'ctx')
- grad_router: float32 [2048, 8], replicated
Inputs may be any that keep to these rules, and one draw needn't show every extreme that they name: `expert_ids`: each token names two different experts. Within one aligned block of 128 tokens no expert is named by more than 40 tokens, and some block reaches 40.
All inputs are finite; a program needn't handle non-finite values.
Results may differ from a plain program's by a relative error of at most 0.013.
The roundings to bfloat16 on the way count: a program that leaves them out, or rounds other values in their place, can miss the bound.
Values may be sent and summed in bfloat16 or wider, within the bound.
A program may use at most 128 MiB of HBM per device.

v0:
```python
import math
import jax
import jax.numpy as jnp
from jax import lax
from jax.sharding import PartitionSpec as P

HEADS = 16
NORM_EPSILON = 1e-06


def rounded(value):
    return lax.optimization_barrier(value.astype(jnp.bfloat16)).astype(jnp.float32)


def contract_rows(left_side, right_side):
    return lax.dot_general(
        left_side, right_side, (((0,), (0,)), ((), ())), preferred_element_type=jnp.float32
    )


def contract_cols(left_side, right_side):
    return lax.dot_general(
        left_side, right_side, (((1,), (1,)), ((), ())), preferred_element_type=jnp.float32
    )


def local(
    resid,
    queries,
    keys,
    values,
    mod_scale,
    mod_shift,
    mod_gate,
    router,
    w_in,
    w_out,
    expert_ids,
    grad_out,
):
    tok_rows, width = resid.shape
    head_size = width // HEADS
    score_scale = 1.0 / math.sqrt(head_size)
    experts = router.shape[1]
    capacity = 5 * tok_rows // (2 * experts)
    groups = lax.axis_size("ctx")
    block_units = w_in.shape[2]
    clip_keys, clip_values = (
        lax.all_gather(keys, "ctx", axis=0, tiled=True),
        lax.all_gather(values, "ctx", axis=0, tiled=True),
    )
    clip_len = clip_keys.shape[0]
    query_heads = queries.reshape(tok_rows, HEADS, head_size)
    key_heads = clip_keys.reshape(clip_len, HEADS, head_size)
    value_heads = clip_values.reshape(clip_len, HEADS, head_size)
    scores = (
        jnp.einsum("qhd,khd->hqk", query_heads, key_heads, preferred_element_type=jnp.float32)
        * score_scale
    )
    row_top = jnp.max(scores, axis=-1)
    exp_scores = jnp.exp(scores - row_top[..., None])
    row_total = jnp.sum(exp_scores, axis=-1)
    mixed_values = jnp.einsum(
        "hqk,khd->qhd",
        exp_scores.astype(jnp.bfloat16),
        value_heads,
        preferred_element_type=jnp.float32,
    )
    attn_heads = (mixed_values / row_total.T[:, :, None]).astype(jnp.bfloat16)
    log_total = row_top + jnp.log(row_total)
    hidden_sum = resid.astype(jnp.float32) + attn_heads.reshape(tok_rows, width).astype(jnp.float32)
    inv_rms = lax.rsqrt(jnp.mean(hidden_sum * hidden_sum, axis=-1, keepdims=True) + NORM_EPSILON)
    normed = hidden_sum * inv_rms
    lift_gain = 1.0 + mod_scale
    normed_mod = (normed * lift_gain + mod_shift).astype(jnp.bfloat16)
    logits = jnp.dot(normed_mod, router, preferred_element_type=jnp.float32)
    expert_range = jnp.arange(experts, dtype=jnp.int32)
    first_hot = (expert_ids[:, 0:1] == expert_range[None, :]).astype(jnp.float32)
    second_hot = (expert_ids[:, 1:2] == expert_range[None, :]).astype(jnp.float32)
    margin = jnp.sum(logits * first_hot, axis=-1) - jnp.sum(logits * second_hot, axis=-1)
    gate_one = jax.nn.sigmoid(margin)
    gate_two = 1.0 - gate_one
    both_hot = first_hot + second_hot
    earlier = jnp.cumsum(both_hot, axis=0) - both_hot
    place_one = expert_ids[:, 0] * capacity + jnp.sum(earlier * first_hot, axis=-1).astype(
        jnp.int32
    )
    place_two = expert_ids[:, 1] * capacity + jnp.sum(earlier * second_hot, axis=-1).astype(
        jnp.int32
    )
    slot_range = jnp.arange(experts * capacity, dtype=jnp.int32)
    pick_one = (place_one[:, None] == slot_range[None, :]).astype(jnp.bfloat16)
    pick_two = (place_two[:, None] == slot_range[None, :]).astype(jnp.bfloat16)
    sent_rows = (
        contract_rows(pick_one + pick_two, normed_mod)
        .astype(jnp.bfloat16)
        .reshape(experts, capacity, width)
    )
    full_in, full_out = (
        lax.all_gather(w_in, "ctx", axis=2, tiled=True),
        lax.all_gather(w_out, "ctx", axis=1, tiled=True),
    )
    full_in = full_in[0]
    full_out = full_out[0]
    arrived = lax.all_to_all(sent_rows, "expert", split_axis=0, concat_axis=0, tiled=True)
    item_count = arrived.shape[1]
    flat_rows = arrived.reshape(-1, width)
    pre_act = jnp.dot(flat_rows, full_in, preferred_element_type=jnp.float32)
    activated = jax.nn.gelu(pre_act).astype(jnp.bfloat16)
    block_sum = jnp.zeros((flat_rows.shape[0], width), jnp.float32)
    for expert_block_index in range(groups):
        expert_low_col = expert_block_index * block_units
        block_sum = block_sum + rounded(
            jnp.dot(
                activated[:, expert_low_col : expert_low_col + block_units],
                full_out[expert_low_col : expert_low_col + block_units],
                preferred_element_type=jnp.float32,
            )
        )
    returned = lax.all_to_all(
        block_sum.astype(jnp.bfloat16).reshape(experts, item_count, width),
        "expert",
        split_axis=0,
        concat_axis=0,
        tiled=True,
    )
    kept_pre = pre_act.reshape(experts, item_count, -1)
    kept_act = activated.reshape(experts, item_count, -1)
    home_flat = returned.reshape(experts * capacity, width)
    result_one = jnp.dot(pick_one, home_flat, preferred_element_type=jnp.float32)
    result_two = jnp.dot(pick_two, home_flat, preferred_element_type=jnp.float32)
    branch = gate_one[:, None] * result_one + gate_two[:, None] * result_two
    mixed_out = (hidden_sum + mod_gate * branch).astype(jnp.bfloat16)
    grad_float = grad_out.astype(jnp.float32)
    branch_grad = mod_gate * grad_float
    grad_one = (gate_one[:, None] * branch_grad).astype(jnp.bfloat16)
    grad_two = (gate_two[:, None] * branch_grad).astype(jnp.bfloat16)
    gate_tilt = (
        (jnp.sum(branch_grad * result_one, axis=-1) - jnp.sum(branch_grad * result_two, axis=-1))
        * gate_one
        * gate_two
    )
    logit_grad = (gate_tilt[:, None] * (first_hot - second_hot)).astype(jnp.bfloat16)
    grad_router = lax.psum(contract_rows(normed_mod, logit_grad), ("expert", "ctx"))
    back_router = contract_cols(logit_grad, router)
    sent_grads = (contract_rows(pick_one, grad_one) + contract_rows(pick_two, grad_two)).astype(
        jnp.bfloat16
    )
    sent_grads = sent_grads.reshape(experts, capacity, width)
    arrived_grads = lax.all_to_all(sent_grads, "expert", split_axis=0, concat_axis=0, tiled=True)
    rows_flat = arrived.reshape(-1, width)
    pre_flat = kept_pre.reshape(-1, kept_pre.shape[2])
    act_flat = kept_act.reshape(-1, kept_act.shape[2])
    gelu_pull = jax.vjp(jax.nn.gelu, pre_flat)[1]
    grad_flat = arrived_grads.reshape(-1, width)
    pre_grad = gelu_pull(contract_cols(grad_flat, full_out))[0].astype(jnp.bfloat16)
    block_sum = jnp.zeros((grad_flat.shape[0], width), jnp.float32)
    for block_index in range(groups):
        low_col = block_index * block_units
        block_sum = block_sum + rounded(
            contract_cols(
                pre_grad[:, low_col : low_col + block_units],
                full_in[:, low_col : low_col + block_units],
            )
        )
    back_rows = lax.all_to_all(
        block_sum.astype(jnp.bfloat16).reshape(experts, capacity, width),
        "expert",
        split_axis=0,
        concat_axis=0,
        tiled=True,
    )
    weight_sums = lax.psum_scatter(
        jnp.concatenate(
            [contract_rows(pre_grad, rows_flat), contract_rows(act_flat, grad_flat)], axis=1
        ).astype(jnp.bfloat16),
        "ctx",
        scatter_dimension=0,
        tiled=True,
    ).astype(jnp.float32)
    grad_w_in = weight_sums[:, :width].T.astype(jnp.bfloat16)[None]
    grad_w_out = weight_sums[:, width:].astype(jnp.bfloat16)[None]
    back_flat = back_rows.reshape(experts * capacity, width)
    input_grad = (
        jnp.dot(pick_one, back_flat, preferred_element_type=jnp.float32)
        + jnp.dot(pick_two, back_flat, preferred_element_type=jnp.float32)
        + back_router
    )
    lifted = input_grad * lift_gain
    resid_grad = grad_float + inv_rms * (
        lifted - normed * jnp.mean(lifted * normed, axis=-1, keepdims=True)
    )
    resid_grad = resid_grad.astype(jnp.bfloat16)
    grad_heads = resid_grad.reshape(tok_rows, HEADS, head_size)
    prob = jnp.exp(scores - log_total[..., None])
    prob_low = prob.astype(jnp.bfloat16)
    value_pull = jnp.einsum(
        "qhd,khd->hqk", grad_heads, value_heads, preferred_element_type=jnp.float32
    )
    row_dot = jnp.einsum("qhd,qhd->hq", grad_heads, attn_heads, preferred_element_type=jnp.float32)
    score_grad = (prob * (value_pull - row_dot[..., None])).astype(jnp.bfloat16)
    grad_queries = (
        (
            jnp.einsum("hqk,khd->qhd", score_grad, key_heads, preferred_element_type=jnp.float32)
            * score_scale
        )
        .astype(jnp.bfloat16)
        .reshape(tok_rows, width)
    )
    row_count = lax.axis_size("ctx") * tok_rows
    key_term = rounded(
        jnp.einsum("hqk,qhd->khd", score_grad, query_heads, preferred_element_type=jnp.float32)
        * score_scale
    )
    value_term = rounded(
        jnp.einsum("hqk,qhd->khd", prob_low, grad_heads, preferred_element_type=jnp.float32)
    )
    key_sums = lax.psum_scatter(
        jnp.concatenate(
            [key_term.reshape(row_count, width), value_term.reshape(row_count, width)], axis=1
        ).astype(jnp.bfloat16),
        "ctx",
        scatter_dimension=0,
        tiled=True,
    ).astype(jnp.float32)
    grad_keys = key_sums[:, :width].astype(jnp.bfloat16)
    grad_values = key_sums[:, width:].astype(jnp.bfloat16)
    return (
        mixed_out,
        resid_grad,
        grad_queries,
        grad_keys,
        grad_values,
        grad_w_in,
        grad_w_out,
        grad_router,
    )


def solution(mesh):
    return jax.shard_map(
        local,
        mesh=mesh,
        in_specs=(
            P(("expert", "ctx"), None),
            P(("expert", "ctx"), None),
            P(("expert", "ctx"), None),
            P(("expert", "ctx"), None),
            P("expert", None),
            P("expert", None),
            P("expert", None),
            P(),
            P("expert", None, "ctx"),
            P("expert", "ctx", None),
            P(("expert", "ctx"), None),
            P(("expert", "ctx"), None),
        ),
        out_specs=(
            P(("expert", "ctx"), None),
            P(("expert", "ctx"), None),
            P(("expert", "ctx"), None),
            P(("expert", "ctx"), None),
            P(("expert", "ctx"), None),
            P("expert", None, "ctx"),
            P("expert", "ctx", None),
            P(),
        ),
        check_vma=False,
    )
```

profile of v0, /device:TPU:1, one launch (start us, length us, event | category | flops | bytes accessed | tf_op | source)
XLA Modules:
  0.0 538.3 jit_solution(17121193874179204365)
XLA Ops:
  11.7 22.9 %all-gather.7.cloned.1.call-done = bf16[512,2048]{1,0:T(8,128)(2,1)} async-done(((bf16[128,2048]{1,0:T(8,128)(2,1)}), bf16[512,2048]{1,0:T(8,128)(2,1)}) %all-gather.7.cloned.1.call-update) | async-done | bytes 2097168 | tf_op jit(solution)/shard_map/all_gather | solution.py:50
  34.6 2.9 copy.54
  37.5 22.1 %all-gather.5.cloned.1.call-done = bf16[512,2048]{0,1:T(8,128)(2,1)} async-done(((bf16[128,2048]{0,1:T(8,128)(2,1)}), bf16[512,2048]{0,1:T(8,128)(2,1)}) %all-gather.5.cloned.1.call-update) | async-done | bytes 2097168 | tf_op jit(solution)/shard_map/all_gather | solution.py:49
  59.6 2.4 multiply_reduce_fusion
  68.5 35.7 %all_to_all.20 = bf16[8,40,2048]{2,1,0:T(8,128)(2,1)} all-to-all(bf16[8,40,2048]{2,1,0:T(8,128)(2,1)S(1)} %bitcast.130), channel_id=1, replica_groups=mesh['expert'=8,'ctx'=4] {'expert'}, dimensions={0} | all-to-all | bytes 2621440 | tf_op jit(solution)/shard_map/all_to_all | solution.py:105
  104.3 6.1 %multiply_convert_fusion.2 = (bf16[320,1024]{1,0:T(8,128)(2,1)S(1)}, f32[320,1024]{1,0:T(8,128)}) fusion(bf16[320,2048]{1,0:T(8,128)(2,1)} %bitcast.140, bf16[1,2048,1024]{2,1,0:T(8,128)(2,1)} %all-gather.9.cloned.1.call-done), kind=kOutput, calls=%fused_computation.55 | convolution fusion | flops 1345126400 | bytes 7471104 | tf_op jit(solution)/shard_map/dot_general | solution.py:108
  110.4 21.7 %all-gather.11.cloned.1.call-done = bf16[1,1024,2048]{2,1,0:T(8,128)(2,1)} async-done(((bf16[1,256,2048]{2,1,0:T(8,128)(2,1)}), bf16[1,1024,2048]{2,1,0:T(8,128)(2,1)}) %all-gather.11.cloned.1.call-update) | async-done | bytes 4194320 | tf_op jit(solution)/shard_map/all_gather | solution.py:101
  137.9 35.8 %all_to_all.21 = bf16[8,40,2048]{2,1,0:T(8,128)(2,1)S(1)} all-to-all(bf16[8,40,2048]{2,1,0:T(8,128)(2,1)S(1)} %bitcast.132), channel_id=1, replica_groups=mesh['expert'=8,'ctx'=4] {'expert'}, dimensions={0} | all-to-all | bytes 2621440 | tf_op jit(solution)/shard_map/all_to_all | solution.py:120
  177.0 34.8 %all_to_all.22 = bf16[8,40,2048]{2,1,0:T(8,128)(2,1)S(1)} all-to-all(bf16[8,40,2048]{2,1,0:T(8,128)(2,1)S(1)} %bitcast.129), channel_id=1, replica_groups=mesh['expert'=8,'ctx'=4] {'expert'}, dimensions={0} | all-to-all | bytes 2621440 | tf_op jit(solution)/shard_map/all_to_all | solution.py:150
  218.7 4.1 all-to-all-start.3
  223.1 29.9 %all-to-all-done.3 = bf16[8,40,2048]{2,1,0:T(8,128)(2,1)S(1)} async-done(((bf16[8,40,2048]{2,1,0:T(8,128)(2,1)}), bf16[8,40,2048]{2,1,0:T(8,128)(2,1)S(1)}, u32[]{:S(2)}, u32[]{:S(2)}) %all-to-all-start.3) | async-done | bytes 1310752 | tf_op jit(solution)/shard_map/all_to_all | solution.py:166
  261.2 4.7 convert_bitcast_fusion
  269.6 3.9 copy.62
  273.5 4.5 pad_maximum_fusion.1
  277.9 6.4 %copy.77 = bf16[512,4096]{1,0:T(8,128)(2,1)} copy(bf16[512,4096]{0,1:T(8,128)(2,1)} %pad_maximum_fusion.1) | data formatting | bytes 8388608
  284.4 6.1 %convolution_convert_fusion.1 = bf16[1024,2048]{1,0:T(8,128)(2,1)} fusion(bf16[320,1024]{1,0:T(8,128)(2,1)} %copy-done.22, bf16[320,2048]{1,0:T(8,128)(2,1)} %bitcast.141), kind=kOutput, calls=%fused_computation.9 | convolution fusion | flops 1344274432 | bytes 6160384 | tf_op jit(solution)/shard_map/dot_general | solution.py:16
  290.5 4.3 convolution_convert_fusion
  294.9 7.9 %pad_maximum_fusion = bf16[1024,4096]{1,0:T(8,128)(2,1)} fusion(bf16[1024,2048]{1,0:T(8,128)(2,1)} %convolution_convert_fusion, bf16[1024,2048]{1,0:T(8,128)(2,1)} %convolution_convert_fusion.1), kind=kLoop, calls=%fused_computation | loop fusion | flops 16777216 | bytes 16777216 | tf_op jit(solution)/shard_map/concatenate | solution.py:174
  304.8 2.3 fusion.32
  308.2 20.3 %reduce-scatter.7.cloned.1.call-done = bf16[128,4096]{1,0:T(8,128)(2,1)} async-done(((bf16[512,4096]{1,0:T(8,128)(2,1)}), bf16[128,4096]{1,0:T(8,128)(2,1)}) %reduce-scatter.7.cloned.1.call-update) | async-done | bytes 1048592
  328.5 2.3 fusion.99
  330.7 71.6 %reduce-scatter.5.cloned.1.call-done = bf16[256,4096]{1,0:T(8,128)(2,1)} async-done(((bf16[1024,4096]{1,0:T(8,128)(2,1)}), bf16[256,4096]{1,0:T(8,128)(2,1)}) %reduce-scatter.5.cloned.1.call-update) | async-done | bytes 2097168 | tf_op jit(solution)/shard_map/reduce_scatter | solution.py:173
  402.3 2.7 slice_bitcast_fusion
  406.3 123.6 %all-reduce.2.cloned.1.call-done = f32[2048,8]{0,1:T(8,128)} async-done(((f32[2048,8]{0,1:T(8,128)}), f32[2048,8]{0,1:T(8,128)}) %all-reduce.2.cloned.1.call-update) | async-done | bytes 65552 | tf_op jit(solution)/shard_map/psum | solution.py:144
  (124 shorter events, 44.7 us)
Async XLA Ops:
  7.2 52.5 %copy-start = (bf16[128,2048]{1,0:T(8,128)(2,1)S(1)}, bf16[128,2048]{1,0:T(8,128)(2,1)}, u32[]{:S(2)}) copy-start(bf16[128,2048]{1,0:T(8,128)(2,1)} %param.13) | copy-start | bytes 1572868
  7.2 4.2 copy-start.27
  7.2 4.2 copy-start.26
  7.2 27.4 %all-gather.7.cloned.1.call-start = ((), (), s32[]{:S(2)}) async-start(), calls=%async_computation.7 | async-start | bytes 2621440 | tf_op jit(solution)/shard_map/all_gather | solution.py:50
  7.9 51.7 %all-gather.5.cloned.1.call-start = ((), (), s32[]{:S(2)}) async-start(), calls=%async_computation.6 | async-start | bytes 2621440 | tf_op jit(solution)/shard_map/all_gather | solution.py:49
  10.1 94.2 %all-gather.9.cloned.1.call-start = ((), (), s32[]{:S(2)}) async-start(), calls=%async_computation.8 | async-start | bytes 5242880 | tf_op jit(solution)/shard_map/all_gather | solution.py:100
  10.8 121.3 %all-gather.11.cloned.1.call-start = ((), (), s32[]{:S(2)}) async-start(), calls=%async_computation.9 | async-start | bytes 5242880 | tf_op jit(solution)/shard_map/all_gather | solution.py:101
  37.5 25.8 %copy-start.6 = (bf16[512,2048]{0,1:T(8,128)(2,1)}, bf16[512,2048]{0,1:T(8,128)(2,1)S(1)}, u32[]{:S(2)}) copy-start(bf16[512,2048]{0,1:T(8,128)(2,1)S(1)} %copy.54) | copy-start | bytes 6291460
  67.7 36.6 %copy-start.10 = (bf16[128,2048]{1,0:T(8,128)(2,1)}, bf16[128,2048]{1,0:T(8,128)(2,1)S(1)}, u32[]{:S(2)}) copy-start(bf16[128,2048]{1,0:T(8,128)(2,1)S(1)} %add_convert_fusion.3) | copy-start | bytes 1572868
  110.4 25.9 %copy-start.20 = (bf16[320,1024]{1,0:T(8,128)(2,1)}, bf16[320,1024]{1,0:T(8,128)(2,1)S(1)}, u32[]{:S(2)}) copy-start(bf16[320,1024]{1,0:T(8,128)(2,1)S(1)} %get-tuple-element.54) | copy-start | bytes 1966084
  132.1 3.6 copy-start.13
  137.8 36.3 %copy-start.8 = (bf16[128,2048]{1,0:T(8,128)(2,1)S(1)}, bf16[128,2048]{1,0:T(8,128)(2,1)}, u32[]{:S(2)}) copy-start(bf16[128,2048]{1,0:T(8,128)(2,1)} %param.23) | copy-start | bytes 1572868
  137.9 36.3 %copy-start.23 = (f32[1,2048]{1,0:T(1,128)S(1)}, f32[1,2048]{1,0:T(1,128)}, u32[]{:S(2)}) copy-start(f32[1,2048]{1,0:T(1,128)} %param.18) | copy-start | bytes 24580
  177.0 34.8 %copy-start.28 = (f32[320,1024]{1,0:T(8,128)S(1)}, f32[320,1024]{1,0:T(8,128)}, u32[]{:S(2)}) copy-start(f32[320,1024]{1,0:T(8,128)} %get-tuple-element.55) | copy-start | bytes 3932164
  211.8 2.7 copy-start.12
  218.7 34.3 %all-to-all-start.3 = ((bf16[8,40,2048]{2,1,0:T(8,128)(2,1)}), bf16[8,40,2048]{2,1,0:T(8,128)(2,1)S(1)}, u32[]{:S(2)}, u32[]{:S(2)}) async-start(bf16[8,40,2048]{2,1,0:T(8,128)(2,1)} %bitcast.131), calls=%async_computation.3 | async-start | bytes 2621440 | tf_op jit(solution)/shard_map/all_to_all | solution.py:166
  222.9 105.6 %reduce-scatter.7.cloned.1.call-start = ((), (), s32[]{:S(2)}) async-start(), calls=%async_computation.12 | async-start | bytes 5242880
  257.3 2.5 copy-start.16
  261.2 4.7 copy-start.2
  261.2 4.7 copy-start.7
  284.3 6.2 %copy-start.21 = (bf16[320,1024]{1,0:T(8,128)(2,1)S(1)}, bf16[320,1024]{1,0:T(8,128)(2,1)}, u32[]{:S(2)}) copy-start(bf16[320,1024]{1,0:T(8,128)(2,1)} %copy-done.20) | copy-start | bytes 1966084
  284.3 118.0 %reduce-scatter.5.cloned.1.call-start = ((), (), s32[]{:S(2)}) async-start(), calls=%async_computation.10 | async-start | bytes 10485760 | tf_op jit(solution)/shard_map/reduce_scatter | solution.py:173
  284.4 6.1 %copy-start.19 = (bf16[8,40,2048]{2,1,0:T(8,128)(2,1)S(1)}, bf16[8,40,2048]{2,1,0:T(8,128)(2,1)}, u32[]{:S(2)}) copy-start(bf16[8,40,2048]{2,1,0:T(8,128)(2,1)} %copy-done.18) | copy-start | bytes 3932164
  302.8 227.1 %all-reduce.2.cloned.1.call-start = ((), (), s32[]{:S(2)}) async-start(), calls=%async_computation.11 | async-start | bytes 131072 | tf_op jit(solution)/shard_map/psum | solution.py:144
  (13 other events, 17.9 us)
Sparse Core Ops, SparseCore 0:
  9.6 25.0 all-gather.6
  36.7 22.8 all-gather.4
  61.2 34.9 all-gather.8
  97.6 34.4 all-gather.10
  284.5 43.9 reduce-scatter.6
  330.9 71.3 reduce-scatter.4
  408.5 121.4 all-reduce.1
where the time goes:
time: 539 us; the launch traced here: 538 us
  waiting for transfers between devices  314 us (58%)
  blocking collectives  106 us (20%)
  matrix products  46.1 us (9%)
  local copies, waits for them, and re-layouts  32.1 us (6%)
  other arithmetic  20.4 us (4%)
  between operations  14.6 us (3%)
    psum x1, waiting for transfers between devices, local(): lax.psum(contract_rows(normed_mod, logit_grad), ('expert', 'ctx'))  124 us
    reduce_scatter x1, waiting for transfers between devices, local(): lax.psum_scatter(jnp.concatenate([contract_rows(pre_grad, rows_flat), con...  71.6 us
    all_to_all x1, blocking collectives, local(): lax.all_to_all(block_sum.astype(jnp.bfloat16).reshape(experts, item_count...  35.8 us
    all_to_all x1, blocking collectives, local(): lax.all_to_all(sent_rows, 'expert', split_axis=0, concat_axis=0, tiled=True)  35.7 us
    all_to_all x1, blocking collectives, local(): lax.all_to_all(sent_grads, 'expert', split_axis=0, concat_axis=0, tiled=T...  34.8 us
    all_to_all x1, waiting for transfers between devices, local(): lax.all_to_all(block_sum.astype(jnp.bfloat16).reshape(experts, capacity,...  29.9 us
    all_gather x1, waiting for transfers between devices, local(): lax.all_gather(values, 'ctx', axis=0, tiled=True)  22.9 us
    unnamed x8, waiting for transfers between devices  22.3 us
  transfers between devices with their start and end apart: 8, of which 7 were waited for; matrix products, arithmetic and copies ran while one was open for 9% of the time, Pallas kernels for 0%

commit v1 on v0

--- a/solution.py
+++ b/solution.py
@@ -3,6 +3,7 @@
 import jax.numpy as jnp
 from jax import lax
 from jax.sharding import PartitionSpec as P
+from jax.lax import all_gather
 
 HEADS = 16
 NORM_EPSILON = 1e-06
@@ -141,7 +142,8 @@
         * gate_two
     )
     logit_grad = (gate_tilt[:, None] * (first_hot - second_hot)).astype(jnp.bfloat16)
-    grad_router = lax.psum(contract_rows(normed_mod, logit_grad), ("expert", "ctx"))
+    view = contract_rows(normed_mod, logit_grad)
+    grad_router = all_gather(view, axis_name=("expert", "ctx")).sum(axis=0)
     back_router = contract_cols(logit_grad, router)
     sent_grads = (contract_rows(pick_one, grad_one) + contract_rows(pick_two, grad_two)).astype(
         jnp.bfloat16

time: 539 us -> 423 us (0.78)
  waiting for transfers between devices: 314 us -> 196 us
    psum x1 -> x0, waiting for transfers between devices: 124 us -> none  [local(): lax.psum(contract_rows(normed_mod, logit_grad), ('expert', 'ctx'))]
    unnamed x8, waiting for transfers between devices: 22.3 us -> 28.9 us
    unnamed x65 -> x60, local copies, waits for them, and re-layouts: 19.4 us -> 16.6 us
  transfers between devices with their start and end apart: 8 -> 8, of which waited for: 7 -> 6; matrix products, arithmetic and copies ran while one was open for 9% -> 18% of each run, Pallas kernels for 0% -> 0%
where the time goes in v1:
time: 423 us; the launch traced here: 421 us
  waiting for transfers between devices  196 us (46%)
  blocking collectives  106 us (25%)
  matrix products  48.6 us (11%)
  local copies, waits for them, and re-layouts  29.3 us (7%)
  other arithmetic  21.3 us (5%)
  between operations  14.6 us (3%)
  starting transfers between devices  4.91 us (1%)
    reduce_scatter x1, waiting for transfers between devices, local(): lax.psum_scatter(jnp.concatenate([contract_rows(pre_grad, rows_flat), con...  71.8 us
    all_to_all x1, blocking collectives, local(): lax.all_to_all(block_sum.astype(jnp.bfloat16).reshape(experts, item_count...  35.8 us
    all_to_all x1, blocking collectives, local(): lax.all_to_all(sent_rows, 'expert', split_axis=0, concat_axis=0, tiled=True)  35.7 us
    all_to_all x1, blocking collectives, local(): lax.all_to_all(sent_grads, 'expert', split_axis=0, concat_axis=0, tiled=T...  34.8 us
    all_to_all x1, waiting for transfers between devices, local(): lax.all_to_all(block_sum.astype(jnp.bfloat16).reshape(experts, capacity,...  29.4 us
    unnamed x8, waiting for transfers between devices  28.9 us
    all_gather x1, waiting for transfers between devices, local(): lax.all_gather(values, 'ctx', axis=0, tiled=True)  22.9 us
    all_gather x1, waiting for transfers between devices, local(): lax.all_gather(keys, 'ctx', axis=0, tiled=True)  22.1 us
  transfers between devices with their start and end apart: 8, of which 6 were waited for; matrix products, arithmetic and copies ran while one was open for 18% of the time, Pallas kernels for 0%

profile of v1, /device:TPU:1, one launch (start us, length us, event | category | flops | bytes accessed | tf_op | source)
XLA Modules:
  0.0 421.1 jit_solution(6660232893982055955)
XLA Ops:
  11.7 22.9 %all-gather.9.cloned.1.call-done = bf16[512,2048]{1,0:T(8,128)(2,1)} async-done(((bf16[128,2048]{1,0:T(8,128)(2,1)}), bf16[512,2048]{1,0:T(8,128)(2,1)}) %all-gather.9.cloned.1.call-update) | async-done | bytes 2097168 | tf_op jit(solution)/shard_map/all_gather | solution.py:51
  34.6 2.9 copy.54
  37.5 22.1 %all-gather.7.cloned.1.call-done = bf16[512,2048]{0,1:T(8,128)(2,1)} async-done(((bf16[128,2048]{0,1:T(8,128)(2,1)}), bf16[512,2048]{0,1:T(8,128)(2,1)}) %all-gather.7.cloned.1.call-update) | async-done | bytes 2097168 | tf_op jit(solution)/shard_map/all_gather | solution.py:50
  59.6 2.4 multiply_reduce_fusion
  69.0 35.7 %all_to_all.20 = bf16[8,40,2048]{2,1,0:T(8,128)(2,1)S(1)} all-to-all(bf16[8,40,2048]{2,1,0:T(8,128)(2,1)S(1)} %bitcast.131), channel_id=1, replica_groups=mesh['expert'=8,'ctx'=4] {'expert'}, dimensions={0} | all-to-all | bytes 2621440 | tf_op jit(solution)/shard_map/all_to_all | solution.py:106
  104.7 6.3 %multiply_convert_fusion.2 = (bf16[320,1024]{1,0:T(8,128)(2,1)}, f32[320,1024]{1,0:T(8,128)}) fusion(bf16[320,2048]{1,0:T(8,128)(2,1)S(1)} %bitcast.142, bf16[1,2048,1024]{2,1,0:T(8,128)(2,1)} %all-gather.11.cloned.1.call-done), kind=kOutput, calls=%fused_computation.55 | convolution fusion | flops 1345126400 | bytes 7471104 | tf_op jit(solution)/shard_map/dot_general | solution.py:109
  111.0 21.1 %all-gather.13.cloned.1.call-done = bf16[1,1024,2048]{2,1,0:T(8,128)(2,1)} async-done(((bf16[1,256,2048]{2,1,0:T(8,128)(2,1)}), bf16[1,1024,2048]{2,1,0:T(8,128)(2,1)}) %all-gather.13.cloned.1.call-update) | async-done | bytes 4194320 | tf_op jit(solution)/shard_map/all_gather | solution.py:102
  137.9 35.8 %all_to_all.21 = bf16[8,40,2048]{2,1,0:T(8,128)(2,1)S(1)} all-to-all(bf16[8,40,2048]{2,1,0:T(8,128)(2,1)S(1)} %bitcast.133), channel_id=1, replica_groups=mesh['expert'=8,'ctx'=4] {'expert'}, dimensions={0} | all-to-all | bytes 2621440 | tf_op jit(solution)/shard_map/all_to_all | solution.py:121
  177.1 34.8 %all_to_all.22 = bf16[8,40,2048]{2,1,0:T(8,128)(2,1)S(1)} all-to-all(bf16[8,40,2048]{2,1,0:T(8,128)(2,1)S(1)} %bitcast.130), channel_id=1, replica_groups=mesh['expert'=8,'ctx'=4] {'expert'}, dimensions={0} | all-to-all | bytes 2621440 | tf_op jit(solution)/shard_map/all_to_all | solution.py:152
  218.8 4.1 all-to-all-start.3
  225.2 29.4 %all-to-all-done.3 = bf16[8,40,2048]{2,1,0:T(8,128)(2,1)S(1)} async-done(((bf16[8,40,2048]{2,1,0:T(8,128)(2,1)}), bf16[8,40,2048]{2,1,0:T(8,128)(2,1)S(1)}, u32[]{:S(2)}, u32[]{:S(2)}) %all-to-all-start.3) | async-done | bytes 1310752 | tf_op jit(solution)/shard_map/all_to_all | solution.py:168
  261.6 4.2 multiply_convert_fusion.1
  268.0 3.9 copy.62
  272.0 3.3 convert_bitcast_fusion
  277.5 6.4 %copy.77 = bf16[512,4096]{1,0:T(8,128)(2,1)} copy(bf16[512,4096]{0,1:T(8,128)(2,1)} %pad_maximum_fusion.1) | data formatting | bytes 8388608
  284.3 5.9 %convolution_convert_fusion.1 = bf16[1024,2048]{1,0:T(8,128)(2,1)} fusion(bf16[320,1024]{1,0:T(8,128)(2,1)} %copy-done.20, bf16[320,2048]{1,0:T(8,128)(2,1)} %bitcast.143), kind=kOutput, calls=%fused_computation.9 | convolution fusion | flops 1344274432 | bytes 6160384 | tf_op jit(solution)/shard_map/dot_general | solution.py:17
  290.3 4.4 %convolution_convert_fusion = bf16[1024,2048]{1,0:T(8,128)(2,1)} fusion(bf16[320,1024]{1,0:T(8,128)(2,1)S(1)} %copy-done.19, bf16[320,2048]{1,0:T(8,128)(2,1)S(1)} %bitcast.145), kind=kOutput, calls=%fused_computation.8 | convolution fusion | flops 1344274432 | bytes 6160384 | tf_op jit(solution)/shard_map/dot_general | solution.py:17
  294.6 9.0 %pad_maximum_fusion = bf16[1024,4096]{1,0:T(8,128)(2,1)} fusion(bf16[1024,2048]{1,0:T(8,128)(2,1)} %convolution_convert_fusion, bf16[1024,2048]{1,0:T(8,128)(2,1)} %convolution_convert_fusion.1), kind=kLoop, calls=%fused_computation | loop fusion | flops 16777216 | bytes 16777216 | tf_op jit(solution)/shard_map/concatenate | solution.py:176
  303.7 2.3 reduce_sum.99
  306.0 2.3 fusion.32
  309.3 26.9 %reduce-scatter.7.cloned.1.call-done = bf16[128,4096]{1,0:T(8,128)(2,1)} async-done(((bf16[512,4096]{1,0:T(8,128)(2,1)}), bf16[128,4096]{1,0:T(8,128)(2,1)}) %reduce-scatter.7.cloned.1.call-update) | async-done | bytes 1048592
  336.2 2.3 fusion.99
  338.5 71.8 %reduce-scatter.5.cloned.1.call-done = bf16[256,4096]{1,0:T(8,128)(2,1)} async-done(((bf16[1024,4096]{1,0:T(8,128)(2,1)}), bf16[256,4096]{1,0:T(8,128)(2,1)}) %reduce-scatter.5.cloned.1.call-update) | async-done | bytes 2097168 | tf_op jit(solution)/shard_map/reduce_scatter | solution.py:175
  410.3 2.7 slice_bitcast_fusion
  (120 shorter events, 43.8 us)
Async XLA Ops:
  7.2 52.5 %copy-start = (bf16[128,2048]{1,0:T(8,128)(2,1)S(1)}, bf16[128,2048]{1,0:T(8,128)(2,1)}, u32[]{:S(2)}) copy-start(bf16[128,2048]{1,0:T(8,128)(2,1)} %param.13) | copy-start | bytes 1572868
  7.2 4.2 copy-start.25
  7.2 4.2 copy-start.24
  7.2 27.4 %all-gather.9.cloned.1.call-start = ((), (), s32[]{:S(2)}) async-start(), calls=%async_computation.7 | async-start | bytes 2621440 | tf_op jit(solution)/shard_map/all_gather | solution.py:51
  7.9 51.7 %all-gather.7.cloned.1.call-start = ((), (), s32[]{:S(2)}) async-start(), calls=%async_computation.6 | async-start | bytes 2621440 | tf_op jit(solution)/shard_map/all_gather | solution.py:50
  10.0 94.7 %all-gather.11.cloned.1.call-start = ((), (), s32[]{:S(2)}) async-start(), calls=%async_computation.8 | async-start | bytes 5242880 | tf_op jit(solution)/shard_map/all_gather | solution.py:101
  10.8 121.3 %all-gather.13.cloned.1.call-start = ((), (), s32[]{:S(2)}) async-start(), calls=%async_computation.9 | async-start | bytes 5242880 | tf_op jit(solution)/shard_map/all_gather | solution.py:102
  37.5 25.8 %copy-start.5 = (bf16[512,2048]{0,1:T(8,128)(2,1)}, bf16[512,2048]{0,1:T(8,128)(2,1)S(1)}, u32[]{:S(2)}) copy-start(bf16[512,2048]{0,1:T(8,128)(2,1)S(1)} %copy.54) | copy-start | bytes 6291460
  104.7 6.3 %copy-start.15 = (bf16[8,40,2048]{2,1,0:T(8,128)(2,1)}, bf16[8,40,2048]{2,1,0:T(8,128)(2,1)S(1)}, u32[]{:S(2)}) copy-start(bf16[8,40,2048]{2,1,0:T(8,128)(2,1)S(1)} %all_to_all.20) | copy-start | bytes 3932164
  132.1 2.0 copy-start.18
  132.1 3.7 copy-start.11
  137.9 36.3 %copy-start.6 = (bf16[128,2048]{1,0:T(8,128)(2,1)S(1)}, bf16[128,2048]{1,0:T(8,128)(2,1)}, u32[]{:S(2)}) copy-start(bf16[128,2048]{1,0:T(8,128)(2,1)} %param.23) | copy-start | bytes 1572868
  137.9 36.3 %copy-start.21 = (f32[1,2048]{1,0:T(1,128)S(1)}, f32[1,2048]{1,0:T(1,128)}, u32[]{:S(2)}) copy-start(f32[1,2048]{1,0:T(1,128)} %param.18) | copy-start | bytes 24580
  177.1 34.8 %copy-start.26 = (f32[320,1024]{1,0:T(8,128)S(1)}, f32[320,1024]{1,0:T(8,128)}, u32[]{:S(2)}) copy-start(f32[320,1024]{1,0:T(8,128)} %get-tuple-element.55) | copy-start | bytes 3932164
  211.9 2.2 copy-start.16
  211.9 2.7 copy-start.10
  214.1 2.1 copy-start.20
  218.8 35.8 %all-to-all-start.3 = ((bf16[8,40,2048]{2,1,0:T(8,128)(2,1)}), bf16[8,40,2048]{2,1,0:T(8,128)(2,1)S(1)}, u32[]{:S(2)}, u32[]{:S(2)}) async-start(bf16[8,40,2048]{2,1,0:T(8,128)(2,1)} %bitcast.132), calls=%async_computation.3 | async-start | bytes 2621440 | tf_op jit(solution)/shard_map/all_to_all | solution.py:168
  222.9 80.7 %all-gather.15.cloned.1.call-start = ((), (), s32[]{:S(2)}) async-start(), calls=%async_computation.11 | async-start | bytes 2162688 | tf_op jit(solution)/shard_map/all_gather | solution.py:146
  224.9 111.4 %reduce-scatter.7.cloned.1.call-start = ((), (), s32[]{:S(2)}) async-start(), calls=%async_computation.12 | async-start | bytes 5242880
  272.0 3.3 copy-start.9
  284.0 6.3 %copy-start.19 = (bf16[320,1024]{1,0:T(8,128)(2,1)S(1)}, bf16[320,1024]{1,0:T(8,128)(2,1)}, u32[]{:S(2)}) copy-start(bf16[320,1024]{1,0:T(8,128)(2,1)} %get-tuple-element.54) | copy-start | bytes 1966084
  284.0 126.3 %reduce-scatter.5.cloned.1.call-start = ((), (), s32[]{:S(2)}) async-start(), calls=%async_computation.10 | async-start | bytes 10485760 | tf_op jit(solution)/shard_map/reduce_scatter | solution.py:175
  284.3 6.0 %copy-start.17 = (bf16[8,40,2048]{2,1,0:T(8,128)(2,1)S(1)}, bf16[8,40,2048]{2,1,0:T(8,128)(2,1)}, u32[]{:S(2)}) copy-start(bf16[8,40,2048]{2,1,0:T(8,128)(2,1)} %copy-done.16) | copy-start | bytes 3932164
  (11 other events, 13.2 us)
Sparse Core Ops, SparseCore 0:
  9.6 25.0 all-gather.8
  36.7 22.8 all-gather.6
  61.2 34.9 all-gather.10
  97.6 34.4 all-gather.12
  226.9 64.0 all-gather.14
  293.3 42.8 reduce-scatter.6
  338.8 71.4 reduce-scatter.4
